TPU v7x, 512 devices: a whole 4x8x8 slice. The times are simulated.
512 devices in a mesh: aux: 32 (over x_lo, y, core), pair: 16 (over z, x_hi).
Axes of the slice: x: 4 (x_hi: 2, x_lo: 2; x = x_hi * 2 + x_lo), y: 8, z: 8, core: 2. Of those that a mesh axis runs over, the one named last changes fastest.
Arguments:
- integrals: bfloat16 [4096, 32, 512], P('aux', 'pair'), may hold values from -0.5 to 0.5
- occ_density: bfloat16 [32, 32], replicated, may hold values from -1 to 1
- virt_density: bfloat16 [512, 512], replicated, may hold values from -0.25 to 0.25
- screen: int32 [64, 32], P('aux', 'pair'), may hold values 0 or 1
Outputs:
- polar: float32 [4096, 4096], P('aux', 'pair')
All inputs are finite; a program needn't handle non-finite values. No bound on the sum of `screen` on one device may be relied on, other than what follows from the above.
Results may differ from a plain program's by a relative error of at most 0.0041.
Values may be sent and summed in bfloat16 or wider, within the bound.
No kernel may reach another device: no remote copies, remote signals or barrier semaphores. Data moves between devices by JAX's collectives and lax.ppermute only.
A program may use at most 64 MiB of HBM per device.

v0:
```python
import jax
import jax.numpy as jnp
from jax import lax
from jax.sharding import PartitionSpec as P


def body(integrals, occ_density, virt_density, screen):
    aux_rows, local_pairs, orbitals = integrals.shape
    blocks = screen.shape[0]
    grouped = integrals.reshape(blocks, aux_rows // blocks, local_pairs, orbitals)
    screened = jnp.where(screen[:, None, :, None] > 0, grouped, jnp.zeros_like(grouped)).reshape(
        aux_rows, local_pairs, orbitals
    )
    column_start = lax.axis_index("pair") * local_pairs
    occ_cols = lax.dynamic_slice_in_dim(occ_density, column_start, local_pairs, 1)
    incoming = lax.all_gather(screened, "pair", axis=1, tiled=True)
    piece_len = incoming.shape[1]
    product = jnp.dot(
        incoming.reshape(aux_rows * piece_len, orbitals),
        virt_density,
        preferred_element_type=jnp.float32,
    )
    virt_piece = product.astype(jnp.bfloat16).reshape(aux_rows, piece_len, orbitals)
    summed = jnp.einsum("pms,ml->pls", virt_piece, occ_cols, preferred_element_type=jnp.float32)
    occupied = summed.astype(jnp.bfloat16).reshape(aux_rows, local_pairs * orbitals)
    incoming = lax.all_gather(screened, "aux", axis=0, tiled=True)
    flat_rows = incoming.reshape(incoming.shape[0], local_pairs * orbitals)
    partial_value = lax.dot_general(
        occupied, flat_rows, (((1,), (1,)), ((), ())), preferred_element_type=jnp.float32
    )
    return lax.psum_scatter(partial_value, "pair", scatter_dimension=1, tiled=True)


def solution(mesh):
    placed = (P("aux", "pair", None), P(), P(), P("aux", "pair"))
    return jax.shard_map(
        body, mesh=mesh, in_specs=placed, out_specs=P("aux", "pair"), check_vma=False
    )
```

profile of v0, /device:TPU:6, one launch (start us, length us, event | category | flops | bytes accessed | tf_op | source)
XLA Modules:
  0.0 422.6 jit_solution(18435790000930779495)
XLA Ops:
  6.5 0.0 copy-start
  6.5 0.0 all-gather.3.cloned.1.call-start
  6.5 0.7 broadcast_compare_fusion
  7.3 0.1 copy.11
  7.4 0.1 broadcast_in_dim.16
  7.5 0.1 broadcast_in_dim.17
  7.6 1.8 copy_select_fusion
  9.3 0.0 all-gather.3.cloned.1.call-update
  9.3 0.0 all-gather.5.cloned.1.call-start
  9.4 0.7 all-gather.5.cloned.1.call-update
  10.1 0.0 reduce-scatter.2.cloned.1.call-start
  10.2 109.5 %all-gather.3.cloned.1.call-done = bf16[128,32,512]{2,0,1:T(8,128)(2,1)} async-done(((bf16[128,2,512]{2,0,1:T(8,128)(2,1)}), bf16[128,32,512]{2,0,1:T(8,128)(2,1)}) %all-gather.3.cloned.1.call-update) | async-done | bytes 4194320 | tf_op jit(solution)/shard_map/all_gather | solution.py:16
  119.7 4.5 %copy.13 = bf16[128,32,512]{2,1,0:T(8,128)(2,1)S(1)} copy(bf16[128,32,512]{2,0,1:T(8,128)(2,1)} %all-gather.3.cloned.1.call-done) | data formatting | bytes 8388608 | tf_op jit(solution)/shard_map/all_gather | solution.py:16
  124.2 0.0 copy-done
  124.2 0.0 copy-start.1
  124.3 2.3 convolution_convert_fusion
  126.6 0.0 copy-done.1
  126.6 0.8 fusion
  127.4 66.5 %all-gather.5.cloned.1.call-done = bf16[4096,2,512]{2,0,1:T(8,128)(2,1)} async-done(((bf16[128,2,512]{2,0,1:T(8,128)(2,1)}), bf16[4096,2,512]{2,0,1:T(8,128)(2,1)}) %all-gather.5.cloned.1.call-update) | async-done | bytes 8388624 | tf_op jit(solution)/shard_map/all_gather | solution.py:26
  193.9 7.5 %convolution_bitcast_fusion = f32[128,4096]{1,0:T(8,128)} fusion(bf16[4096,2,512]{2,0,1:T(8,128)(2,1)} %all-gather.5.cloned.1.call-done, bf16[128,2,512]{2,1,0:T(2,128)(2,1)S(1)} %fusion), kind=kOutput, calls=%fused_computation.1 | convolution fusion | flops 1073741824 | bytes 10747904 | tf_op jit(solution)/shard_map/dot_general | solution.py:28
  201.5 0.0 reduce-scatter.2.cloned.1.call-update
  201.5 214.6 %reduce-scatter.2.cloned.1.call-done = f32[128,256]{1,0:T(8,128)} async-done(((f32[128,4096]{1,0:T(8,128)}), f32[128,256]{1,0:T(8,128)}) %reduce-scatter.2.cloned.1.call-update) | async-done | bytes 131088 | tf_op jit(solution)/shard_map/reduce_scatter | solution.py:31
Async XLA Ops:
  6.5 117.7 %copy-start = (bf16[512,512]{1,0:T(8,128)(2,1)S(1)}, bf16[512,512]{1,0:T(8,128)(2,1)}, u32[]{:S(2)}) copy-start(bf16[512,512]{1,0:T(8,128)(2,1)} %param.6) | copy-start | bytes 1572868
  6.5 113.2 %all-gather.3.cloned.1.call-start = ((), (), s32[]{:S(2)}) async-start(), calls=%async_computation.1 | async-start | bytes 4456448 | tf_op jit(solution)/shard_map/all_gather | solution.py:16
  9.3 184.6 %all-gather.5.cloned.1.call-start = ((), (), s32[]{:S(2)}) async-start(), calls=%async_computation.2 | async-start | bytes 8650752 | tf_op jit(solution)/shard_map/all_gather | solution.py:26
  10.1 406.0 %reduce-scatter.2.cloned.1.call-start = ((), (), s32[]{:S(2)}) async-start(), calls=%async_computation.3 | async-start | bytes 2228224 | tf_op jit(solution)/shard_map/reduce_scatter | solution.py:31
  124.2 2.4 copy-start.1
Sparse Core Ops, SparseCore 0:
  10.5 109.1 all-gather.2
  121.9 72.0 all-gather.4
  201.6 214.4 reduce-scatter.1
where the time goes:
time: 424 us; the launch traced here: 423 us
  waiting for transfers between devices  391 us (92%)
  between operations  13.1 us (3%)
  matrix products  10.7 us (3%)
  local copies, waits for them, and re-layouts  4.81 us (1%)
    reduce_scatter x1, waiting for transfers between devices, body(): lax.psum_scatter(partial_value, 'pair', scatter_dimension=1, tiled=True)  215 us
    all_gather x1, waiting for transfers between devices, body(): incoming = lax.all_gather(screened, 'pair', axis=1, tiled=True)  110 us
    all_gather x1, waiting for transfers between devices, body(): incoming = lax.all_gather(screened, 'aux', axis=0, tiled=True)  66.5 us
  transfers between devices with their start and end apart: 3, of which 3 were waited for; matrix products, arithmetic and copies ran while one was open for 2% of the time, Pallas kernels for 0%

commit v1 on v0

v1 whole, which is shorter than its diff:
```python
import jax
import jax.numpy as jnp
from jax import lax
from jax.sharding import Mesh, PartitionSpec as P

AUX = ("x_lo", "y", "core")
PAIR = ("z", "x_hi")
PLANE = ("x_lo", "core", "z", "x_hi")
WIDE = ("x_lo", "core", "x_hi")


def exchange(values):
    pieces = values.reshape(2, 2, 2, 16, 2, 8, 64)
    pieces = pieces.transpose(0, 1, 5, 2, 3, 4, 6).reshape(64, 16, 128)
    got = lax.all_to_all(pieces, PLANE, 0, 0, tiled=True)
    got = got.reshape(4, 16, 16, 128).transpose(0, 2, 1, 3)
    return got.reshape(64, 2048)


def body(integrals, occ_density, virt_density, screen):
    aux_rows, local_pairs, orbitals = integrals.shape
    blocks = screen.shape[0]
    grouped = integrals.reshape(blocks, aux_rows // blocks, local_pairs, orbitals)
    screened = jnp.where(screen[:, None, :, None] > 0, grouped, jnp.zeros_like(grouped)).reshape(
        aux_rows, local_pairs, orbitals
    )
    virtual = jnp.dot(
        screened.reshape(aux_rows * local_pairs, orbitals),
        virt_density,
        preferred_element_type=jnp.float32,
    ).astype(jnp.bfloat16).reshape(aux_rows, local_pairs, orbitals)
    mine = exchange(screened)
    columns = lax.all_gather(mine, "y", axis=0, tiled=True)
    virt_rows = exchange(virtual).reshape(64, 32, 64)
    occupied = jnp.einsum("pms,ml->pls", virt_rows, occ_density, preferred_element_type=jnp.float32)
    occupied = occupied.astype(jnp.bfloat16).reshape(64, 2048)
    rows = lax.all_gather(occupied, WIDE, axis=0, tiled=True)
    rows = rows.reshape(8, 4, 16, 2048).transpose(1, 0, 2, 3).reshape(512, 2048)
    part = lax.dot_general(columns, rows, (((1,), (1,)), ((), ())), preferred_element_type=jnp.float32)
    part = part.astype(jnp.bfloat16)
    tiles = part.reshape(4, 2, 2, 32, 2, 2, 128).transpose(4, 5, 2, 0, 1, 3, 6).reshape(64, 32, 128)
    got = lax.all_to_all(tiles, PLANE, 0, 0, tiled=True)
    total = jnp.sum(got.reshape(2, 2, 8, 2, 2, 16, 128).astype(jnp.float32), axis=2)
    return total.transpose(5, 3, 0, 1, 2, 4).reshape(128, 256)


def solution(mesh):
    fine = Mesh(mesh.devices.reshape(2, 8, 2, 8, 2), AUX + PAIR)
    placed = (P(AUX, PAIR, None), P(), P(), P(AUX, PAIR))
    return jax.shard_map(body, mesh=fine, in_specs=placed, out_specs=P(AUX, PAIR), check_vma=False)
```

time: 424 us -> 189 us (0.45)
  waiting for transfers between devices: 391 us -> 88 us
  blocking collectives: 0 us -> 73.9 us
  matrix products: 10.7 us -> 3.54 us
    reduce_scatter x1 -> x0, waiting for transfers between devices: 215 us -> none  [body(): lax.psum_scatter(partial_value, 'pair', scatter_dimension=1, tiled=True)]
    all_gather x2, waiting for transfers between devices: 176 us -> 88 us  [the longest x1 51.8 us: body(): columns = lax.all_gather(mine, 'y', axis=0, tiled=True)]
    all_to_all x0 -> x3, blocking collectives: none -> 73.9 us  [the longest x2 44.6 us: exchange(): got = lax.all_to_all(pieces, PLANE, 0, 0, tiled=True)]
    dot_general x3, matrix products: 10.7 us -> 3.54 us  [the longest x1 2.87 us: body(): lax.dot_general(columns, rows, (((1,), (1,)), ((), ())), preferred_elemen...]
    all_gather x1 -> x0, local copies, waits for them, and re-layouts: 4.53 us -> none  [body(): incoming = lax.all_gather(screened, 'pair', axis=1, tiled=True)]
  transfers between devices with their start and end apart: 3 -> 2, of which waited for: 3 -> 2; matrix products, arithmetic and copies ran while one was open for 2% -> 2% of each run, Pallas kernels for 0% -> 0%
where the time goes in v1:
time: 189 us; the launch traced here: 188 us
  waiting for transfers between devices  88 us (47%)
  blocking collectives  73.9 us (39%)
  between operations  13.6 us (7%)
  local copies, waits for them, and re-layouts  7.99 us (4%)
  matrix products  3.54 us (2%)
    all_gather x1, waiting for transfers between devices, body(): columns = lax.all_gather(mine, 'y', axis=0, tiled=True)  51.8 us
    all_to_all x2, blocking collectives, exchange(): got = lax.all_to_all(pieces, PLANE, 0, 0, tiled=True)  44.6 us
    all_gather x1, waiting for transfers between devices, body(): rows = lax.all_gather(occupied, WIDE, axis=0, tiled=True)  36.2 us
    all_to_all x1, blocking collectives, body(): got = lax.all_to_all(tiles, PLANE, 0, 0, tiled=True)  29.3 us
  transfers between devices with their start and end apart: 2, of which 2 were waited for; matrix products, arithmetic and copies ran while one was open for 2% of the time, Pallas kernels for 0%

profile of v1, /device:TPU:6, one launch (start us, length us, event | category | flops | bytes accessed | tf_op | source)
XLA Modules:
  0.0 188.4 jit_solution(10271872201832409334)
XLA Ops:
  6.5 0.0 copy-start
  6.5 0.0 all-gather.5.cloned.1.call-start
  6.5 0.7 broadcast_compare_fusion
  7.3 0.1 broadcast_in_dim.23
  7.4 1.1 reshape.50
  8.5 0.0 copy-done
  8.5 0.3 convolution_convert_fusion.2
  8.9 0.0 copy-start.2
  8.9 0.3 reshape_reshape.8
  9.2 0.5 copy.36
  9.7 0.3 reshape.51
  10.0 0.0 copy-start.1
  10.0 26.7 %all_to_all.15 = bf16[64,16,128]{2,1,0:T(8,128)(2,1)S(1)} all-to-all(bf16[64,16,128]{2,1,0:T(8,128)(2,1)S(1)} %reshape.51), channel_id=1, replica_groups=mesh['x_lo'=2,'y'=8,'core'=2,'z'=8,'x_hi'=2] {'x_lo','core','z','x_hi'}, dimensions={0} | all-to-all | bytes 524288 | tf_op jit(solution)/shard_map/all_to_all | solution.py:15
  36.7 0.1 copy.24
  36.7 0.2 reshape_reshape.9
  37.0 0.0 copy-done.2
  37.0 0.3 fusion
  37.3 1.2 reshape.53
  38.5 0.0 all-gather.5.cloned.1.call-update
  38.6 0.0 all-gather.3.cloned.1.call-start
  38.6 0.0 copy-done.1
  38.6 0.3 reshape.46
  39.0 0.6 fusion.1
  39.5 0.3 reshape.47
  39.8 17.9 %all_to_all.16 = bf16[64,16,128]{2,1,0:T(8,128)(2,1)S(1)} all-to-all(bf16[64,16,128]{2,1,0:T(8,128)(2,1)S(1)} %reshape.47), channel_id=1, replica_groups=mesh['x_lo'=2,'y'=8,'core'=2,'z'=8,'x_hi'=2] {'x_lo','core','z','x_hi'}, dimensions={0} | all-to-all | bytes 524288 | tf_op jit(solution)/shard_map/all_to_all | solution.py:15
  57.8 0.1 copy.22
  57.8 0.8 copy.37
  58.6 0.0 all-gather.3.cloned.1.call-update
  58.6 36.2 %all-gather.5.cloned.1.call-done = bf16[512,2048]{1,0:T(8,128)(2,1)} async-done(((bf16[64,2048]{1,0:T(8,128)(2,1)}), bf16[512,2048]{1,0:T(8,128)(2,1)}) %all-gather.5.cloned.1.call-update) | async-done | bytes 2097168 | tf_op jit(solution)/shard_map/all_gather | solution.py:37
  94.9 1.7 copy.26
  96.6 51.8 %all-gather.3.cloned.1.call-done = bf16[512,2048]{1,0:T(8,128)(2,1)} async-done(((bf16[64,2048]{1,0:T(8,128)(2,1)}), bf16[512,2048]{1,0:T(8,128)(2,1)}) %all-gather.3.cloned.1.call-update) | async-done | bytes 2097168 | tf_op jit(solution)/shard_map/all_gather | solution.py:33
  148.4 2.9 %convolution_convert_fusion = bf16[512,512]{1,0:T(8,128)(2,1)S(1)} fusion(bf16[512,2048]{1,0:T(8,128)(2,1)} %all-gather.3.cloned.1.call-done, bf16[512,2048]{1,0:T(8,128)(2,1)S(1)} %bitcast.39), kind=kOutput, calls=%fused_computation | convolution fusion | flops 1074003968 | bytes 4718592 | tf_op jit(solution)/shard_map/dot_general | solution.py:39
  151.2 0.1 reshape.56
  151.4 0.1 copy.27
  151.5 29.3 %all_to_all.17 = bf16[64,32,128]{2,1,0:T(8,128)(2,1)S(1)} all-to-all(bf16[64,32,128]{2,1,0:T(8,128)(2,1)S(1)} %bitcast.41), channel_id=1, replica_groups=mesh['x_lo'=2,'y'=8,'core'=2,'z'=8,'x_hi'=2] {'x_lo','core','z','x_hi'}, dimensions={0} | all-to-all | bytes 1048576 | tf_op jit(solution)/shard_map/all_to_all | solution.py:42
  180.7 0.1 convert_reduce_fusion
  180.8 0.8 copy.29
  (2 shorter events, 0.0 us)
Async XLA Ops:
  6.5 2.0 %copy-start = (bf16[512,512]{1,0:T(8,128)(2,1)S(1)}, bf16[512,512]{1,0:T(8,128)(2,1)}, u32[]{:S(2)}) copy-start(bf16[512,512]{1,0:T(8,128)(2,1)} %param.6) | copy-start | bytes 1572868
  6.5 88.3 %all-gather.5.cloned.1.call-start = ((), (), s32[]{:S(2)}) async-start(), calls=%async_computation.4 | async-start | bytes 2359296 | tf_op jit(solution)/shard_map/all_gather | solution.py:37
  8.9 28.1 %copy-start.2 = (bf16[32,32]{1,0:T(8,128)(2,1)S(1)}, bf16[32,32]{1,0:T(8,128)(2,1)}, u32[]{:S(2)}) copy-start(bf16[32,32]{1,0:T(8,128)(2,1)} %param.5) | copy-start | bytes 6148
  10.0 28.6 %copy-start.1 = (bf16[128,2,512]{2,1,0:T(2,128)(2,1)S(1)}, bf16[128,2,512]{2,1,0:T(2,128)(2,1)}, u32[]{:S(2)}) copy-start(bf16[128,2,512]{2,1,0:T(2,128)(2,1)} %param.4) | copy-start | bytes 786436
  38.6 109.8 %all-gather.3.cloned.1.call-start = ((), (), s32[]{:S(2)}) async-start(), calls=%async_computation.3 | async-start | bytes 2359296 | tf_op jit(solution)/shard_map/all_gather | solution.py:33
Sparse Core Ops, SparseCore 0:
  38.7 56.1 all-gather.4
  96.9 51.3 all-gather.2
